TPU v7x, 32 devices: a whole 2x2x4 slice. The times are simulated.
32 devices in a mesh: ctx: 8 (over z, y), wt: 4 (over x, core).
Axes of the slice: x: 2, y: 2, z: 4, core: 2. Of those that a mesh axis runs over, the one named last changes fastest.
Arguments:
- layer_input: bfloat16 [4, 1024, 1024], P('wt', 'ctx'), may hold values from -6 to 6
- out_grad: bfloat16 [4, 1024, 1024], P('wt', 'ctx'), may hold values from -6 to 6
- deal: int32 [8, 2], replicated, may hold values from 0 to 15, as said below
- w_qkv: bfloat16 [1024, 3072], P('wt'), may hold values from -0.1875 to 0.1875
- w_out: bfloat16 [1024, 1024], P('wt'), may hold values from -0.1875 to 0.1875
- w_up: bfloat16 [1024, 4096], P('wt'), may hold values from -0.1875 to 0.1875
- w_down: bfloat16 [4096, 1024], P('wt'), may hold values from -0.09375 to 0.09375
- norm_gain: bfloat16 [4, 1024], P(None, 'wt'), may hold values from 0.099609375 to 1.8984375
- norm_shift: bfloat16 [4, 1024], P(None, 'wt'), may hold values from -1.5 to 1.5
- bias_width: bfloat16 [4, 1024], P(None, 'wt'), may hold values from -2.5 to 2.5
- up_bias: bfloat16 [4096], P('wt'), may hold values from -2.5 to 2.5
Outputs:
- layer_out: bfloat16 [4, 1024, 1024], P('wt', 'ctx')
- input_grad: float32 [4, 1024, 1024], P('wt', 'ctx')
- grad_qkv: float32 [1024, 3072], P('wt')
- grad_out: float32 [1024, 1024], P('wt')
- grad_up: float32 [1024, 4096], P('wt')
- grad_down: float32 [4096, 1024], P('wt')
- grad_gain: float32 [4, 1024], P(None, 'wt')
- grad_shift: float32 [4, 1024], P(None, 'wt')
- grad_bias: float32 [4, 1024], P(None, 'wt')
- grad_up_bias: float32 [4096], P('wt')
Inputs may be any that keep to these rules, and one draw needn't show every extreme that they name: `deal`: pieces of 64 tokens are numbered along a sequence. Row j holds a number p below 8 and its mirror 1024 // 64 - 1 - p; every piece appears once.
All inputs are finite; a program needn't handle non-finite values.
Results may differ from a plain program's by a relative error of at most 0.015.
Values may be sent and summed in bfloat16 or wider, within the bound.
No kernel may reach another device: no remote copies, remote signals or barrier semaphores. Data moves between devices by JAX's collectives and lax.ppermute only.
A program may use at most 320 MiB of HBM per device.

v0:
```python
import math
import jax
import jax.numpy as jnp
from jax import lax
from jax.sharding import PartitionSpec as P

HEADS = 16
BLK = 256
PIECE = 64
epsilon = 1e-05
relax = 32.0


def layer_norm(value, gain, shift):
    mean = jnp.mean(value, axis=-1, keepdims=True)
    centered = value - mean
    spread = jnp.mean(centered * centered, axis=-1, keepdims=True)
    return centered * lax.rsqrt(spread + epsilon) * gain + shift


def gelu_tanh(value):
    return jax.nn.gelu(value, approximate=True)


def rows_dot(left, weight):
    return jnp.einsum("std,de->ste", left, weight, preferred_element_type=jnp.float32)


def weight_grad(left, right):
    return jnp.einsum("std,ste->de", left, right, preferred_element_type=jnp.float32)


def back_dot(grad, weight):
    return jnp.einsum("ste,de->std", grad, weight, preferred_element_type=jnp.float32)


def row_total(value):
    return jnp.sum(value.astype(jnp.float32), axis=(0, 1))


def per_device(
    layer_input,
    out_grad,
    deal,
    w_qkv,
    w_out,
    w_up,
    w_down,
    norm_gain,
    norm_shift,
    bias_width,
    up_bias,
):
    seqs, rows, width = layer_input.shape
    heads = HEADS
    head = width // heads
    prescale = 1.0 / (relax * math.sqrt(head))
    ranks = lax.axis_size("ctx")
    length = rows * ranks
    per_block = BLK // PIECE
    rank = lax.axis_index("ctx")
    chosen = jnp.arange(ranks, dtype=jnp.int32) == rank
    mine = jnp.sum(jnp.where(chosen[:, None], deal, 0), axis=0)
    query_blocks = jnp.repeat(mine, rows // 2) // per_block
    key_blocks = jnp.repeat(deal.reshape(-1), rows // 2) // per_block
    full_qkv, full_out, full_up, full_down, gains, shifts, biases, up_shift = (
        lax.all_gather(w_qkv, "wt", axis=0, tiled=True),
        lax.all_gather(w_out, "wt", axis=0, tiled=True),
        lax.all_gather(w_up, "wt", axis=0, tiled=True),
        lax.all_gather(w_down, "wt", axis=0, tiled=True),
        lax.all_gather(norm_gain, "wt", axis=1, tiled=True),
        lax.all_gather(norm_shift, "wt", axis=1, tiled=True),
        lax.all_gather(bias_width, "wt", axis=1, tiled=True),
        lax.all_gather(up_bias, "wt", axis=0, tiled=True),
    )
    gains = gains.astype(jnp.float32)
    shifts = shifts.astype(jnp.float32)
    biases = biases.astype(jnp.float32)
    up_shift = up_shift.astype(jnp.float32)
    input_float = layer_input.astype(jnp.float32)
    first = layer_norm(input_float, gains[0], shifts[0]).astype(jnp.bfloat16)
    mixed = rows_dot(first, full_qkv)
    query = (mixed[..., :width] + biases[0]).astype(jnp.bfloat16)
    kv_local = jnp.concatenate(
        [mixed[..., width : 2 * width], mixed[..., 2 * width :] + biases[1]], axis=-1
    ).astype(jnp.bfloat16)
    kv_all = lax.all_gather(kv_local, "ctx", axis=1, tiled=True)
    step = math.gcd(length, 1024)
    count = length // step
    query4 = query.reshape(seqs, rows, heads, head)

    def score_block(left, right):
        return (
            jnp.einsum("sqhd,skhd->shqk", left, right, preferred_element_type=jnp.float32)
            * prescale
        )

    def key_block(index):
        start = index * step
        piece = lax.dynamic_slice_in_dim(kv_all, start, step, 1)
        keys4 = piece[..., :width].reshape(seqs, step, heads, head)
        values4 = piece[..., width:].reshape(seqs, step, heads, head)
        visible = (
            query_blocks[:, None] >= lax.dynamic_slice_in_dim(key_blocks, start, step, 0)[None, :]
        )
        return (keys4, values4, visible)

    def probs(raw, visible, totals):
        return jnp.where(visible, jnp.exp(raw * relax - totals[..., None]), 0.0)

    def online(index, carry):
        top, total, acc = carry
        keys4, values4, visible = key_block(index)
        raw = jnp.where(visible, score_block(query4, keys4), -1e30)
        new_top = jnp.maximum(top, jnp.max(raw, axis=-1))
        terms = jnp.where(visible, jnp.exp((raw - new_top[..., None]) * relax), 0.0)
        factor = jnp.exp((top - new_top) * relax)
        total = total * factor + jnp.sum(terms, axis=-1)
        acc = acc * jnp.transpose(factor, (0, 2, 1))[..., None]
        acc = acc + jnp.einsum(
            "shqk,skhd->sqhd",
            terms.astype(jnp.bfloat16),
            values4,
            preferred_element_type=jnp.float32,
        )
        return (new_top, total, acc)

    start_top = jnp.full((seqs, heads, rows), -1e30, jnp.float32)
    start_total = jnp.zeros((seqs, heads, rows), jnp.float32)
    start_acc = jnp.zeros((seqs, rows, heads, head), jnp.float32)
    top, total, acc = lax.fori_loop(0, count, online, (start_top, start_total, start_acc))
    log_total = top * relax + jnp.log(total)
    attended_float = acc / jnp.transpose(total, (0, 2, 1))[..., None]
    attended = attended_float.reshape(seqs, rows, width).astype(jnp.bfloat16)
    branch = rows_dot(attended, full_out) + biases[2]
    resid = input_float + layer_norm(branch, gains[1], shifts[1])
    second = layer_norm(resid, gains[2], shifts[2]).astype(jnp.bfloat16)
    upper = rows_dot(second, full_up) + up_shift
    hidden = gelu_tanh(upper).astype(jnp.bfloat16)
    ffn = rows_dot(hidden, full_down) + biases[3]
    top_norm, pull_four = jax.vjp(layer_norm, ffn, gains[3], shifts[3])
    result = resid + top_norm
    d_out = out_grad.astype(jnp.float32)
    d_ffn, d_gain3, d_shift3 = pull_four(d_out)
    d_ffn = d_ffn.astype(jnp.bfloat16)
    d_bias3 = row_total(d_ffn)
    g_down = weight_grad(hidden, d_ffn)
    d_hidden = back_dot(d_ffn, full_down)
    _, pull_gelu = jax.vjp(gelu_tanh, upper)
    d_upper = pull_gelu(d_hidden)[0].astype(jnp.bfloat16)
    d_up_shift = row_total(d_upper)
    g_up = weight_grad(second, d_upper)
    d_second = back_dot(d_upper, full_up)
    _, pull_three = jax.vjp(layer_norm, resid, gains[2], shifts[2])
    d_resid_part, d_gain2, d_shift2 = pull_three(d_second)
    d_resid = d_out + d_resid_part
    _, pull_two = jax.vjp(layer_norm, branch, gains[1], shifts[1])
    d_branch, d_gain1, d_shift1 = pull_two(d_resid)
    d_branch = d_branch.astype(jnp.bfloat16)
    d_bias2 = row_total(d_branch)
    g_out = weight_grad(attended, d_branch)
    d_attended = back_dot(d_branch, full_out).astype(jnp.bfloat16)
    d_out4 = d_attended.reshape(seqs, rows, heads, head)
    delta = jnp.einsum("sqhd,sqhd->shq", d_out4.astype(jnp.float32), attended_float)

    def score_grads(q_rows, do_rows, k_rows, v_rows, visible, lse_rows, delta_rows):
        weights = probs(score_block(q_rows, k_rows), visible, lse_rows)
        d_probs = jnp.einsum("sqhd,skhd->shqk", do_rows, v_rows, preferred_element_type=jnp.float32)
        d_scores = (relax * weights * (d_probs - delta_rows[..., None])).astype(jnp.bfloat16)
        return (d_scores, weights.astype(jnp.bfloat16))

    zero_query = jnp.zeros((seqs, rows, heads, head), jnp.float32)

    def local_grads(d_query, index):
        keys4, values4, visible = key_block(index)
        d_scores, weights = score_grads(query4, d_out4, keys4, values4, visible, log_total, delta)
        d_query = (
            d_query
            + jnp.einsum("shqk,skhd->sqhd", d_scores, keys4, preferred_element_type=jnp.float32)
            * prescale
        )
        d_keys = (
            jnp.einsum("shqk,sqhd->kshd", d_scores, query4, preferred_element_type=jnp.float32)
            * prescale
        )
        d_values = jnp.einsum(
            "shqk,sqhd->kshd", weights, d_out4, preferred_element_type=jnp.float32
        )
        joined = jnp.concatenate(
            [d_keys.reshape(step, seqs, width), d_values.reshape(step, seqs, width)], axis=-1
        )
        return (d_query, joined)

    d_query, pieces = lax.scan(local_grads, zero_query, jnp.arange(count, dtype=jnp.int32))
    terms = pieces.reshape(length, seqs, 2 * width)
    d_kv = jnp.transpose(lax.psum_scatter(terms, "ctx", scatter_dimension=0, tiled=True), (1, 0, 2))
    d_query = d_query.reshape(seqs, rows, width).astype(jnp.bfloat16)
    d_kv = d_kv.astype(jnp.bfloat16)
    d_bias0 = row_total(d_query)
    d_bias1 = row_total(d_kv[..., width:])
    d_mixed = jnp.concatenate([d_query, d_kv], axis=-1)
    g_qkv = weight_grad(first, d_mixed)
    d_first = back_dot(d_mixed, full_qkv)
    _, pull_one = jax.vjp(layer_norm, input_float, gains[0], shifts[0])
    d_input_part, d_gain0, d_shift0 = pull_one(d_first)
    input_grad = d_resid + d_input_part
    grad_gain = jnp.stack([d_gain0, d_gain1, d_gain2, d_gain3])
    grad_shift = jnp.stack([d_shift0, d_shift1, d_shift2, d_shift3])
    grad_bias = jnp.stack([d_bias0, d_bias1, d_bias2, d_bias3])
    owned = (
        lax.psum_scatter(g_qkv.astype(jnp.bfloat16), "wt", scatter_dimension=0, tiled=True).astype(
            jnp.float32
        ),
        lax.psum_scatter(g_out.astype(jnp.bfloat16), "wt", scatter_dimension=0, tiled=True).astype(
            jnp.float32
        ),
        lax.psum_scatter(g_up.astype(jnp.bfloat16), "wt", scatter_dimension=0, tiled=True).astype(
            jnp.float32
        ),
        lax.psum_scatter(g_down.astype(jnp.bfloat16), "wt", scatter_dimension=0, tiled=True).astype(
            jnp.float32
        ),
        lax.psum_scatter(
            grad_gain.astype(jnp.bfloat16), "wt", scatter_dimension=1, tiled=True
        ).astype(jnp.float32),
        lax.psum_scatter(
            grad_shift.astype(jnp.bfloat16), "wt", scatter_dimension=1, tiled=True
        ).astype(jnp.float32),
        lax.psum_scatter(
            grad_bias.astype(jnp.bfloat16), "wt", scatter_dimension=1, tiled=True
        ).astype(jnp.float32),
        lax.psum_scatter(
            d_up_shift.astype(jnp.bfloat16), "wt", scatter_dimension=0, tiled=True
        ).astype(jnp.float32),
    )
    summed = lax.psum(
        (owned[0], owned[1], owned[2], owned[3], owned[4], owned[5], owned[6], owned[7]), "ctx"
    )
    return (
        result.astype(jnp.bfloat16),
        input_grad,
        summed[0],
        summed[1],
        summed[2],
        summed[3],
        summed[4],
        summed[5],
        summed[6],
        summed[7],
    )


def solution(mesh):
    in_specs = (
        P("wt", "ctx", None),
        P("wt", "ctx", None),
        P(),
        P("wt", None),
        P("wt", None),
        P("wt", None),
        P("wt", None),
        P(None, "wt"),
        P(None, "wt"),
        P(None, "wt"),
        P("wt"),
    )
    out_specs = (
        P("wt", "ctx", None),
        P("wt", "ctx", None),
        P("wt", None),
        P("wt", None),
        P("wt", None),
        P("wt", None),
        P(None, "wt"),
        P(None, "wt"),
        P(None, "wt"),
        P("wt"),
    )
    return jax.shard_map(
        per_device, mesh=mesh, in_specs=in_specs, out_specs=out_specs, check_vma=False
    )
```

profile of v0, /device:TPU:0, one launch (start us, length us, event | category | flops | bytes accessed | tf_op | source)
XLA Modules:
  0.0 1275.9 jit_solution(7949901151484038611)
XLA Ops:
  8.0 6.3 all_gather.30
  14.2 5.5 all_gather.28
  19.7 5.3 all_gather.27
  29.1 29.6 %all-gather.6.cloned.1.call-done = bf16[1024,3072]{1,0:T(8,128)(2,1)} async-done(((bf16[256,3072]{1,0:T(8,128)(2,1)}), bf16[1024,3072]{1,0:T(8,128)(2,1)}) %all-gather.6.cloned.1.call-update) | async-done | bytes 6291472 | tf_op jit(solution)/shard_map/all_gather | solution.py:67
  58.7 4.0 convolution_bitcast_fusion
  65.7 5.2 all_gather.34
  72.4 64.9 %all-gather.8.cloned.1.call-done = bf16[1,1024,2048]{2,1,0:T(8,128)(2,1)} async-done(((bf16[1,128,2048]{2,1,0:T(8,128)(2,1)}), bf16[1,1024,2048]{2,1,0:T(8,128)(2,1)}) %all-gather.8.cloned.1.call-update) | async-done | bytes 4194320 | tf_op jit(solution)/shard_map/all_gather | solution.py:87
  137.3 4.7 fusion.90
  145.4 3.9 copy.38
  165.5 54.0 %all-gather.12.cloned.1.call-done = bf16[1024,4096]{1,0:T(8,128)(2,1)} async-done(((bf16[256,4096]{1,0:T(8,128)(2,1)}), bf16[1024,4096]{1,0:T(8,128)(2,1)}) %all-gather.12.cloned.1.call-update) | async-done | bytes 8388624 | tf_op jit(solution)/shard_map/all_gather | solution.py:69
  219.5 6.1 convolution_add_fusion
  225.6 53.7 %all-gather.14.cloned.1.call-done = bf16[4096,1024]{1,0:T(8,128)(2,1)} async-done(((bf16[1024,1024]{1,0:T(8,128)(2,1)}), bf16[4096,1024]{1,0:T(8,128)(2,1)}) %all-gather.14.cloned.1.call-update) | async-done | bytes 8388624 | tf_op jit(solution)/shard_map/all_gather | solution.py:70
  279.2 5.8 fusion.96
  287.8 4.7 fusion.98
  302.6 4.7 fusion.4
  307.3 5.8 multiply_convert_fusion
  315.1 4.1 pad_maximum_fusion
  322.2 7.0 convolution_convert_fusion.1
  330.2 7.2 convolution_convert_fusion
  338.7 3.9 fusion.97
  342.6 126.1 %reduce-scatter.15.cloned.1.call-done = f32[128,1,2048]{0,2,1:T(8,128)} async-done(((f32[1024,1,2048]{0,2,1:T(8,128)}), f32[128,1,2048]{0,2,1:T(8,128)}) %reduce-scatter.15.cloned.1.call-update) | async-done | bytes 1048592 | tf_op jit(solution)/shard_map/reduce_scatter | solution.py:196
  470.1 5.1 fusion.43
  478.7 4.6 convolution_convert_fusion.2
  485.2 7.3 all-reduce
  492.6 10.0 reduce-scatter.19.cloned.1.call-done
  502.6 74.4 %reduce-scatter.21.cloned.1.call-done = bf16[256,4096]{1,0:T(8,128)(2,1)} async-done(((bf16[1024,4096]{1,0:T(8,128)(2,1)}), bf16[256,4096]{1,0:T(8,128)(2,1)}) %reduce-scatter.21.cloned.1.call-update) | async-done | bytes 2097168 | tf_op jit(solution)/shard_map/reduce_scatter | solution.py:217
  577.0 74.5 %reduce-scatter.23.cloned.1.call-done = bf16[1024,1024]{1,0:T(8,128)(2,1)} async-done(((bf16[4096,1024]{1,0:T(8,128)(2,1)}), bf16[1024,1024]{1,0:T(8,128)(2,1)}) %reduce-scatter.23.cloned.1.call-update) | async-done | bytes 2097168 | tf_op jit(solution)/shard_map/reduce_scatter | solution.py:220
  652.5 21.9 %reduce-scatter.25.cloned.1.call-done = bf16[256,4]{1,0:T(8,128)(2,1)} async-done(((bf16[1024,4]{1,0:T(8,128)(2,1)}), bf16[256,4]{1,0:T(8,128)(2,1)}) %reduce-scatter.25.cloned.1.call-update) | async-done | bytes 2064
  675.4 22.4 %reduce-scatter.27.cloned.1.call-done = bf16[256,4]{1,0:T(8,128)(2,1)} async-done(((bf16[1024,4]{1,0:T(8,128)(2,1)}), bf16[256,4]{1,0:T(8,128)(2,1)}) %reduce-scatter.27.cloned.1.call-update) | async-done | bytes 2064
  698.6 22.0 %reduce-scatter.29.cloned.1.call-done = bf16[256,4]{1,0:T(8,128)(2,1)} async-done(((bf16[1024,4]{1,0:T(8,128)(2,1)}), bf16[256,4]{1,0:T(8,128)(2,1)}) %reduce-scatter.29.cloned.1.call-update) | async-done | bytes 2064
  721.6 60.2 %reduce-scatter.17.cloned.1.call-done = bf16[256,3072]{1,0:T(8,128)(2,1)} async-done(((bf16[1024,3072]{1,0:T(8,128)(2,1)}), bf16[256,3072]{1,0:T(8,128)(2,1)}) %reduce-scatter.17.cloned.1.call-update) | async-done | bytes 1572880 | tf_op jit(solution)/shard_map/reduce_scatter | solution.py:211
  781.8 487.4 %all-reduce.3 = (f32[256,3072]{1,0:T(8,128)}, f32[256,1024]{1,0:T(8,128)}, f32[256,4096]{1,0:T(8,128)}, f32[1024,1024]{1,0:T(8,128)}, f32[4,256]{1,0:T(4,128)}, ...) all-reduce(bf16[256,3072]{1,0:T(8,128)(2,1)} %reduce-scatter.17.clo, ...), channel_id=1, replica_groups=mesh['ctx'=8,'wt'=4] {'ctx'}, use_global_device_ids=true, to_apply=%region_21.22 | all-reduce | flops 3149824 | bytes 18900992 | tf_op jit(solution)/shard_map/psum | solution.py:236
  (235 shorter events, 58.4 us)
Async XLA Ops:
  7.2 51.6 %all-gather.6.cloned.1.call-start = ((), (), s32[]{:S(2)}) async-start(), calls=%async_computation.8 | async-start | bytes 7864320 | tf_op jit(solution)/shard_map/all_gather | solution.py:67
  7.9 129.4 %all-gather.8.cloned.1.call-start = ((), (), s32[]{:S(2)}) async-start(), calls=%async_computation.9 | async-start | bytes 4718592 | tf_op jit(solution)/shard_map/all_gather | solution.py:87
  26.1 32.6 %copy-start.23 = (f32[128]{0:T(128)}, f32[128]{0:T(128)S(1)}, u32[]{:S(2)}) copy-start(f32[128]{0:T(128)S(1)} %broadcast_multiply_fusion.3) | copy-start | bytes 1540
  27.3 31.5 %copy-start.46 = (f32[128]{0:T(128)}, f32[128]{0:T(128)S(1)}, u32[]{:S(2)}) copy-start(f32[128]{0:T(128)S(1)} %fusion.42) | copy-start | bytes 1540
  27.3 31.4 %copy-start.25 = (f32[128]{0:T(128)}, f32[128]{0:T(128)S(1)}, u32[]{:S(2)}) copy-start(f32[128]{0:T(128)S(1)} %fusion.67) | copy-start | bytes 1540
  62.7 8.8 copy-start.44
  63.7 96.0 %all-gather.10.cloned.1.call-start = ((), (), s32[]{:S(2)}) async-start(), calls=%async_computation.10 | async-start | bytes 2621440 | tf_op jit(solution)/shard_map/all_gather | solution.py:68
  64.5 155.0 %all-gather.12.cloned.1.call-start = ((), (), s32[]{:S(2)}) async-start(), calls=%async_computation.11 | async-start | bytes 10485760 | tf_op jit(solution)/shard_map/all_gather | solution.py:69
  65.1 214.2 %all-gather.14.cloned.1.call-start = ((), (), s32[]{:S(2)}) async-start(), calls=%async_computation.12 | async-start | bytes 10485760 | tf_op jit(solution)/shard_map/all_gather | solution.py:70
  65.6 403.2 %reduce-scatter.15.cloned.1.call-start = ((), (), s32[]{:S(2)}) async-start(), calls=%async_computation.13 | async-start | bytes 9437184 | tf_op jit(solution)/shard_map/reduce_scatter | solution.py:196
  72.4 76.9 %copy-start.12 = (bf16[1,128,1024]{1,2,0:T(8,128)(2,1)}, bf16[1,128,1024]{1,2,0:T(8,128)(2,1)S(1)}, u32[]{:S(2)}) copy-start(bf16[1,128,1024]{1,2,0:T(8,128)(2,1)S(1)} %copy.36) | copy-start | bytes 786436
  154.5 8.1 copy-start.1
  279.2 8.5 slice-start.2
  279.2 6.0 copy-start.10
  279.2 6.0 copy-start.21
  279.2 6.8 copy-start.32
  279.2 8.5 slice-start.3
  287.1 5.4 slice-start
  302.5 4.8 copy-start.15
  302.6 4.8 copy-start.22
  307.3 5.8 copy-start.13
  319.2 183.4 %reduce-scatter.19.cloned.1.call-start = ((), (), s32[]{:S(2)}) async-start(), calls=%async_computation.15 | async-start | bytes 2621440 | tf_op jit(solution)/shard_map/reduce_scatter | solution.py:214
  322.2 254.8 %reduce-scatter.21.cloned.1.call-start = ((), (), s32[]{:S(2)}) async-start(), calls=%async_computation.16 | async-start | bytes 10485760 | tf_op jit(solution)/shard_map/reduce_scatter | solution.py:217
  329.3 322.2 %reduce-scatter.23.cloned.1.call-start = ((), (), s32[]{:S(2)}) async-start(), calls=%async_computation.17 | async-start | bytes 10485760 | tf_op jit(solution)/shard_map/reduce_scatter | solution.py:220
  337.5 337.0 %reduce-scatter.25.cloned.1.call-start = ((), (), s32[]{:S(2)}) async-start(), calls=%async_computation.18 | async-start | bytes 327680
  338.6 131.5 %copy-start.24 = (f32[128]{0:T(128)S(1)}, f32[128]{0:T(128)}, u32[]{:S(2)}) copy-start(f32[128]{0:T(128)} %copy-done.23) | copy-start | bytes 1540
  470.1 5.1 copy-start.47
  470.1 5.2 copy-start.26
  476.7 221.0 %reduce-scatter.27.cloned.1.call-start = ((), (), s32[]{:S(2)}) async-start(), calls=%async_computation.19 | async-start | bytes 327680
  477.7 243.0 %reduce-scatter.29.cloned.1.call-start = ((), (), s32[]{:S(2)}) async-start(), calls=%async_computation.20 | async-start | bytes 327680
  478.7 303.1 %reduce-scatter.17.cloned.1.call-start = ((), (), s32[]{:S(2)}) async-start(), calls=%async_computation.14 | async-start | bytes 7864320 | tf_op jit(solution)/shard_map/reduce_scatter | solution.py:211
  483.3 168.2 %copy-start.8 = (f32[1,128,1024]{2,1,0:T(8,128)S(1)}, f32[1,128,1024]{2,1,0:T(8,128)}, u32[]{:S(2)}) copy-start(f32[1,128,1024]{2,1,0:T(8,128)} %copy-done.7) | copy-start | bytes 1572868
  (38 other events, 90.9 us)
Sparse Core Ops, SparseCore 0:
  9.6 49.1 all-gather.5
  63.9 73.4 all-gather.7
  138.9 20.8 all-gather.9
  161.2 58.2 all-gather.11
  220.9 58.2 all-gather.13
  319.3 149.4 reduce-scatter.14
  472.1 30.4 reduce-scatter.18
  505.2 71.7 reduce-scatter.20
  579.7 71.7 reduce-scatter.22
  654.4 20.0 reduce-scatter.24
  677.6 20.0 reduce-scatter.26
  700.6 20.0 reduce-scatter.28
  723.4 58.3 reduce-scatter.16
where the time goes:
time: 1280 us
  waiting for transfers between devices  618 us (48%)
  blocking collectives  517 us (40%)
  matrix products  74.1 us (6%)
  local copies, waits for them, and re-layouts  28.4 us (2%)
  other arithmetic  22.6 us (2%)
  between operations  15.6 us (1%)
    psum x1, blocking collectives, per_device(): lax.psum((owned[0], owned[1], owned[2], owned[3], owned[4], owned[5], own...  487 us
    reduce_scatter x1, waiting for transfers between devices, per_device(): lax.psum_scatter(terms, 'ctx', scatter_dimension=0, tiled=True)  126 us
    reduce_scatter x1, waiting for transfers between devices, per_device(): lax.psum_scatter(g_down.astype(jnp.bfloat16), 'wt', scatter_dimension=0,...  74.5 us
    reduce_scatter x1, waiting for transfers between devices, per_device(): lax.psum_scatter(g_up.astype(jnp.bfloat16), 'wt', scatter_dimension=0, ti...  74.4 us
    unnamed x16, waiting for transfers between devices  68.9 us
    all_gather x1, waiting for transfers between devices, per_device(): kv_all = lax.all_gather(kv_local, 'ctx', axis=1, tiled=True)  64.9 us
    reduce_scatter x1, waiting for transfers between devices, per_device(): lax.psum_scatter(g_qkv.astype(jnp.bfloat16), 'wt', scatter_dimension=0, t...  60.2 us
    all_gather x1, waiting for transfers between devices, per_device(): lax.all_gather(w_up, 'wt', axis=0, tiled=True)  54 us
  transfers between devices with their start and end apart: 13, of which 13 were waited for; matrix products, arithmetic and copies ran while one was open for 6% of the time, Pallas kernels for 0%

commit v1 on v0

--- a/solution.py
+++ b/solution.py
@@ -84,7 +84,15 @@
     kv_local = jnp.concatenate(
         [mixed[..., width : 2 * width], mixed[..., 2 * width :] + biases[1]], axis=-1
     ).astype(jnp.bfloat16)
-    kv_all = lax.all_gather(kv_local, "ctx", axis=1, tiled=True)
+    ways, here = (lax.axis_size("ctx"), lax.axis_index("ctx"))
+    grown, reach = (kv_local, 1)
+    while reach < ways:
+        theirs = lax.ppermute(grown, "ctx", [(d, d ^ reach) for d in range(ways)])
+        mine_first = jnp.concatenate([grown, theirs], axis=1)
+        theirs_first = jnp.concatenate([theirs, grown], axis=1)
+        grown = jnp.where(here & reach == 0, mine_first, theirs_first)
+        reach = 2 * reach
+    kv_all = grown
     step = math.gcd(length, 1024)
     count = length // step
     query4 = query.reshape(seqs, rows, heads, head)

time: 1280 us -> 1240 us (0.969)
  waiting for transfers between devices: 618 us -> 562 us
    ppermute x0 -> x3, waiting for transfers between devices: none -> 118 us  [per_device(): theirs = lax.ppermute(grown, 'ctx', [(d, d ^ reach) for d in range(ways)])]
    all_gather x1 -> x0, waiting for transfers between devices: 64.9 us -> none  [per_device(): kv_all = lax.all_gather(kv_local, 'ctx', axis=1, tiled=True)]
    all_gather x1, waiting for transfers between devices: 54 us -> 0.01 us  [per_device(): lax.all_gather(w_up, 'wt', axis=0, tiled=True)]
    all_gather x1, waiting for transfers between devices: 53.7 us -> 0.01 us  [per_device(): lax.all_gather(w_down, 'wt', axis=0, tiled=True)]
    unnamed x16 -> x15, waiting for transfers between devices: 68.9 us -> 69.2 us
  transfers between devices with their start and end apart: 13 -> 15, of which waited for: 13 -> 12; matrix products, arithmetic and copies ran while one was open for 6% -> 7% of each run, Pallas kernels for 0% -> 0%
where the time goes in v1:
time: 1240 us; the launch traced here: 1230 us
  waiting for transfers between devices  562 us (45%)
  blocking collectives  517 us (42%)
  matrix products  74 us (6%)
  other arithmetic  29.7 us (2%)
  local copies, waits for them, and re-layouts  25.8 us (2%)
  between operations  16 us (1%)
    psum x1, blocking collectives, per_device(): lax.psum((owned[0], owned[1], owned[2], owned[3], owned[4], owned[5], own...  487 us
    reduce_scatter x1, waiting for transfers between devices, per_device(): lax.psum_scatter(terms, 'ctx', scatter_dimension=0, tiled=True)  126 us
    ppermute x3, waiting for transfers between devices, per_device(): theirs = lax.ppermute(grown, 'ctx', [(d, d ^ reach) for d in range(ways)])  118 us
    reduce_scatter x1, waiting for transfers between devices, per_device(): lax.psum_scatter(g_down.astype(jnp.bfloat16), 'wt', scatter_dimension=0,...  74.5 us
    reduce_scatter x1, waiting for transfers between devices, per_device(): lax.psum_scatter(g_up.astype(jnp.bfloat16), 'wt', scatter_dimension=0, ti...  74.3 us
    unnamed x15, waiting for transfers between devices  69.2 us
    reduce_scatter x1, waiting for transfers between devices, per_device(): lax.psum_scatter(g_qkv.astype(jnp.bfloat16), 'wt', scatter_dimension=0, t...  60 us
    all_gather x1, waiting for transfers between devices, per_device(): lax.all_gather(w_qkv, 'wt', axis=0, tiled=True)  29.8 us
  transfers between devices with their start and end apart: 15, of which 12 were waited for; matrix products, arithmetic and copies ran while one was open for 7% of the time, Pallas kernels for 0%

profile of v1, /device:TPU:0, one launch (start us, length us, event | category | flops | bytes accessed | tf_op | source)
XLA Modules:
  0.0 1229.8 jit_solution(4886631883845805506)
XLA Ops:
  10.1 6.1 all_gather.27
  16.2 5.4 all_gather.25
  21.6 5.2 all_gather.24
  29.0 29.8 %all-gather.5.cloned.1.call-done = bf16[1024,3072]{1,0:T(8,128)(2,1)} async-done(((bf16[256,3072]{1,0:T(8,128)(2,1)}), bf16[1024,3072]{1,0:T(8,128)(2,1)}) %all-gather.5.cloned.1.call-update) | async-done | bytes 6291472 | tf_op jit(solution)/shard_map/all_gather | solution.py:67
  58.7 3.9 convolution_bitcast_fusion
  65.8 12.8 %collective-permute-done = bf16[1,128,2048]{2,1,0:T(8,128)(2,1)S(1)} collective-permute-done((bf16[1,128,2048]{2,1,0:T(8,128)(2,1)}, bf16[1,128,2048]{2,1,0:T(8,128)(2,1)S(1)}, u32[]{:S(2)}, u32[]{:S(2)}) %collective-permute-start) | collective-permute-done | bytes 524320 | tf_op jit(solution)/shard_map/ppermute | solution.py:90
  81.6 23.1 %collective-permute-done.1 = bf16[1,256,2048]{2,1,0:T(8,128)(2,1)S(1)} collective-permute-done((bf16[1,256,2048]{2,1,0:T(8,128)(2,1)}, bf16[1,256,2048]{2,1,0:T(8,128)(2,1)S(1)}, u32[]{:S(2)}, u32[]{:S(2)}) %collective-permute-start.1) | collective-permute-done | bytes 1048608 | tf_op jit(solution)/shard_map/ppermute | solution.py:90
  109.4 5.2 all_gather.30
  117.1 82.3 %collective-permute-done.2 = bf16[1,512,2048]{2,1,0:T(8,128)(2,1)} collective-permute-done((bf16[1,512,2048]{2,1,0:T(8,128)(2,1)}, bf16[1,512,2048]{2,1,0:T(8,128)(2,1)}, u32[]{:S(2)}, u32[]{:S(2)}) %collective-permute-start.2) | collective-permute-done | bytes 2097184 | tf_op jit(solution)/shard_map/ppermute | solution.py:90
  199.4 4.2 maximum_select_fusion
  209.0 3.9 copy.38
  227.0 6.1 convolution_add_fusion
  233.1 5.8 fusion.97
  241.7 4.7 fusion.99
  256.4 4.7 fusion.4
  261.2 5.8 multiply_convert_fusion
  269.0 4.1 pad_maximum_fusion
  276.3 6.9 convolution_convert_fusion.1
  284.2 7.2 convolution_convert_fusion
  292.7 3.9 fusion.98
  296.7 126.0 %reduce-scatter.15.cloned.1.call-done = f32[128,1,2048]{0,2,1:T(8,128)} async-done(((f32[1024,1,2048]{0,2,1:T(8,128)}), f32[128,1,2048]{0,2,1:T(8,128)}) %reduce-scatter.15.cloned.1.call-update) | async-done | bytes 1048592 | tf_op jit(solution)/shard_map/reduce_scatter | solution.py:204
  423.9 5.1 fusion.44
  432.5 4.6 convolution_convert_fusion.2
  439.1 7.3 all-reduce
  446.4 9.9 reduce-scatter.19.cloned.1.call-done
  456.3 74.3 %reduce-scatter.21.cloned.1.call-done = bf16[256,4096]{1,0:T(8,128)(2,1)} async-done(((bf16[1024,4096]{1,0:T(8,128)(2,1)}), bf16[256,4096]{1,0:T(8,128)(2,1)}) %reduce-scatter.21.cloned.1.call-update) | async-done | bytes 2097168 | tf_op jit(solution)/shard_map/reduce_scatter | solution.py:225
  530.6 74.5 %reduce-scatter.23.cloned.1.call-done = bf16[1024,1024]{1,0:T(8,128)(2,1)} async-done(((bf16[4096,1024]{1,0:T(8,128)(2,1)}), bf16[1024,1024]{1,0:T(8,128)(2,1)}) %reduce-scatter.23.cloned.1.call-update) | async-done | bytes 2097168 | tf_op jit(solution)/shard_map/reduce_scatter | solution.py:228
  606.1 22.1 %reduce-scatter.25.cloned.1.call-done = bf16[256,4]{1,0:T(8,128)(2,1)} async-done(((bf16[1024,4]{1,0:T(8,128)(2,1)}), bf16[256,4]{1,0:T(8,128)(2,1)}) %reduce-scatter.25.cloned.1.call-update) | async-done | bytes 2064
  629.1 22.2 %reduce-scatter.27.cloned.1.call-done = bf16[256,4]{1,0:T(8,128)(2,1)} async-done(((bf16[1024,4]{1,0:T(8,128)(2,1)}), bf16[256,4]{1,0:T(8,128)(2,1)}) %reduce-scatter.27.cloned.1.call-update) | async-done | bytes 2064
  652.2 22.2 %reduce-scatter.29.cloned.1.call-done = bf16[256,4]{1,0:T(8,128)(2,1)} async-done(((bf16[1024,4]{1,0:T(8,128)(2,1)}), bf16[256,4]{1,0:T(8,128)(2,1)}) %reduce-scatter.29.cloned.1.call-update) | async-done | bytes 2064
  675.3 60.0 %reduce-scatter.17.cloned.1.call-done = bf16[256,3072]{1,0:T(8,128)(2,1)} async-done(((bf16[1024,3072]{1,0:T(8,128)(2,1)}), bf16[256,3072]{1,0:T(8,128)(2,1)}) %reduce-scatter.17.cloned.1.call-update) | async-done | bytes 1572880 | tf_op jit(solution)/shard_map/reduce_scatter | solution.py:219
  735.4 487.4 %all-reduce.3 = (f32[256,3072]{1,0:T(8,128)}, f32[256,1024]{1,0:T(8,128)}, f32[256,4096]{1,0:T(8,128)}, f32[1024,1024]{1,0:T(8,128)}, f32[4,256]{1,0:T(4,128)}, ...) all-reduce(bf16[256,3072]{1,0:T(8,128)(2,1)} %reduce-scatter.17.clo, ...), channel_id=1, replica_groups=mesh['ctx'=8,'wt'=4] {'ctx'}, use_global_device_ids=true, to_apply=%region_21.22 | all-reduce | flops 3149824 | bytes 18900992 | tf_op jit(solution)/shard_map/psum | solution.py:244
  (261 shorter events, 67.5 us)
Async XLA Ops:
  7.2 51.6 %all-gather.5.cloned.1.call-start = ((), (), s32[]{:S(2)}) async-start(), calls=%async_computation.8 | async-start | bytes 7864320 | tf_op jit(solution)/shard_map/all_gather | solution.py:67
  7.9 214.1 %all-gather.7.cloned.1.call-start = ((), (), s32[]{:S(2)}) async-start(), calls=%async_computation.9 | async-start | bytes 2621440 | tf_op jit(solution)/shard_map/all_gather | solution.py:68
  8.7 7.5 copy-start.51
  8.7 12.9 %copy-start.52 = (bf16[4,256]{1,0:T(4,128)(2,1)S(1)}, bf16[4,256]{1,0:T(4,128)(2,1)}, u32[]{:S(2)}) copy-start(bf16[4,256]{1,0:T(4,128)(2,1)} %param.18) | copy-start | bytes 6148
  8.7 18.1 %copy-start.1 = (bf16[1,128,1024]{2,1,0:T(8,128)(2,1)S(1)}, bf16[1,128,1024]{2,1,0:T(8,128)(2,1)}, u32[]{:S(2)}) copy-start(bf16[1,128,1024]{2,1,0:T(8,128)(2,1)} %param.11) | copy-start | bytes 786436
  8.7 218.3 %all-gather.9.cloned.1.call-start = ((), (), s32[]{:S(2)}) async-start(), calls=%async_computation.10 | async-start | bytes 10485760 | tf_op jit(solution)/shard_map/all_gather | solution.py:69
  9.4 223.6 %all-gather.11.cloned.1.call-start = ((), (), s32[]{:S(2)}) async-start(), calls=%async_computation.11 | async-start | bytes 10485760 | tf_op jit(solution)/shard_map/all_gather | solution.py:70
  10.0 412.6 %reduce-scatter.15.cloned.1.call-start = ((), (), s32[]{:S(2)}) async-start(), calls=%async_computation.12 | async-start | bytes 9437184 | tf_op jit(solution)/shard_map/reduce_scatter | solution.py:204
  26.9 31.9 %copy-start.26 = (f32[128]{0:T(128)}, f32[128]{0:T(128)S(1)}, u32[]{:S(2)}) copy-start(f32[128]{0:T(128)S(1)} %broadcast_multiply_fusion.3) | copy-start | bytes 1540
  27.1 31.6 %copy-start.28 = (f32[128]{0:T(128)}, f32[128]{0:T(128)S(1)}, u32[]{:S(2)}) copy-start(f32[128]{0:T(128)S(1)} %fusion.68) | copy-start | bytes 1540
  64.3 14.3 %collective-permute-start = (bf16[1,128,2048]{2,1,0:T(8,128)(2,1)}, bf16[1,128,2048]{2,1,0:T(8,128)(2,1)S(1)}, u32[]{:S(2)}, u32[]{:S(2)}) collective-permute-start(bf16[1,128,2048]{2,1,0:T(8,128)(2,1)} %pad_maximum_fusion.1), channel_id=1, source_target_pairs={{0,4},{4,0},{8,12},{12,8},{16,20},{20,16},{24,28},{28,24},{1,5},{5... | collective-permute-start | bytes 1572872 | tf_op jit(solution)/shard_map/ppermute | solution.py:90
  79.8 24.8 %collective-permute-start.1 = (bf16[1,256,2048]{2,1,0:T(8,128)(2,1)}, bf16[1,256,2048]{2,1,0:T(8,128)(2,1)S(1)}, u32[]{:S(2)}, u32[]{:S(2)}) collective-permute-start(bf16[1,256,2048]{2,1,0:T(8,128)(2,1)} %maximum_select_fusion.4), channel_id=1, source_target_pairs={{0,8},{4,12},{8,0},{12,4},{16,24},{20,28},{24,16},{28,20},{1,9},{5... | collective-permute-start | bytes 3145736 | tf_op jit(solution)/shard_map/ppermute | solution.py:90
  104.7 10.5 copy-start.49
  104.7 11.3 copy-start.20
  107.0 92.4 %collective-permute-start.2 = (bf16[1,512,2048]{2,1,0:T(8,128)(2,1)}, bf16[1,512,2048]{2,1,0:T(8,128)(2,1)}, u32[]{:S(2)}, u32[]{:S(2)}) collective-permute-start(bf16[1,512,2048]{2,1,0:T(8,128)(2,1)} %maximum_select_fusion.2), channel_id=1, source_target_pairs={{0,16},{4,20},{8,24},{12,28},{16,0},{20,4},{24,8},{28,12},{1,17},{... | collective-permute-start | bytes 6291464 | tf_op jit(solution)/shard_map/ppermute | solution.py:90
  116.1 96.8 %copy-start.12 = (bf16[1,128,1024]{1,2,0:T(8,128)(2,1)}, bf16[1,128,1024]{1,2,0:T(8,128)(2,1)S(1)}, u32[]{:S(2)}) copy-start(bf16[1,128,1024]{1,2,0:T(8,128)(2,1)S(1)} %copy.36) | copy-start | bytes 786436
  233.1 8.5 slice-start.2
  233.1 6.0 copy-start.10
  233.1 6.0 copy-start.24
  233.1 6.8 copy-start.35
  233.1 8.5 slice-start.3
  261.2 5.8 copy-start.13
  273.1 183.2 %reduce-scatter.19.cloned.1.call-start = ((), (), s32[]{:S(2)}) async-start(), calls=%async_computation.14 | async-start | bytes 2621440 | tf_op jit(solution)/shard_map/reduce_scatter | solution.py:222
  276.0 254.5 %reduce-scatter.21.cloned.1.call-start = ((), (), s32[]{:S(2)}) async-start(), calls=%async_computation.15 | async-start | bytes 10485760 | tf_op jit(solution)/shard_map/reduce_scatter | solution.py:225
  283.3 321.8 %reduce-scatter.23.cloned.1.call-start = ((), (), s32[]{:S(2)}) async-start(), calls=%async_computation.16 | async-start | bytes 10485760 | tf_op jit(solution)/shard_map/reduce_scatter | solution.py:228
  291.5 336.7 %reduce-scatter.25.cloned.1.call-start = ((), (), s32[]{:S(2)}) async-start(), calls=%async_computation.17 | async-start | bytes 327680
  292.7 131.2 %copy-start.27 = (f32[128]{0:T(128)S(1)}, f32[128]{0:T(128)}, u32[]{:S(2)}) copy-start(f32[128]{0:T(128)} %copy-done.26) | copy-start | bytes 1540
  430.5 220.8 %reduce-scatter.27.cloned.1.call-start = ((), (), s32[]{:S(2)}) async-start(), calls=%async_computation.18 | async-start | bytes 327680
  431.5 242.9 %reduce-scatter.29.cloned.1.call-start = ((), (), s32[]{:S(2)}) async-start(), calls=%async_computation.19 | async-start | bytes 327680
  432.5 302.9 %reduce-scatter.17.cloned.1.call-start = ((), (), s32[]{:S(2)}) async-start(), calls=%async_computation.13 | async-start | bytes 7864320 | tf_op jit(solution)/shard_map/reduce_scatter | solution.py:219
  437.2 167.9 %copy-start.8 = (f32[1,128,1024]{2,1,0:T(8,128)S(1)}, f32[1,128,1024]{2,1,0:T(8,128)}, u32[]{:S(2)}) copy-start(f32[1,128,1024]{2,1,0:T(8,128)} %copy-done.7) | copy-start | bytes 1572868
  456.3 279.1 %copy-start.21 = (bf16[256,1024]{1,0:T(8,128)(2,1)S(1)}, bf16[256,1024]{1,0:T(8,128)(2,1)}, u32[]{:S(2)}) copy-start(bf16[256,1024]{1,0:T(8,128)(2,1)} %reduce-scatter.19.cloned.1.call-done) | copy-start | bytes 1572868
  (48 other events, 124.1 us)
Sparse Core Ops, SparseCore 0:
  9.6 49.1 all-gather.4
  60.3 22.5 all-gather.6
  84.5 58.3 all-gather.8
  144.3 58.2 all-gather.10
  273.2 149.3 reduce-scatter.14
  425.7 30.4 reduce-scatter.18
  458.8 71.6 reduce-scatter.20
  533.3 71.6 reduce-scatter.22
  608.1 20.0 reduce-scatter.24
  631.2 20.0 reduce-scatter.26
  654.3 20.0 reduce-scatter.28
  677.0 58.3 reduce-scatter.16
